TPU v7x, 32 devices: a whole 2x2x4 slice. The times are simulated.
32 devices in a mesh: energy: 16 (over z, y, x), space: 2 (over core).
Axes of the slice: x: 2, y: 2, z: 4, core: 2. Of those that a mesh axis runs over, the one named last changes fastest.
Arguments:
- lesser: bfloat16 [32, 2, 2, 256, 256], P('energy', 'space'), may hold values from -6 to 6
- greater: bfloat16 [32, 2, 2, 256, 256], P('energy', 'space'), may hold values from -6 to 6
- coulomb_diag: bfloat16 [2, 256, 256], P('space'), may hold values from -0.375 to 0.375
- coulomb_upper: bfloat16 [2, 256, 256], P('space'), may hold values from -0.375 to 0.375
Outputs:
- screened: bfloat16 [32, 2, 2, 256, 256], P('energy', 'space')
All inputs are finite; a program needn't handle non-finite values.
Results may differ from a plain program's by a relative error of at most 0.015.
Values may be sent and summed in bfloat16 or wider, within the bound.
A program may use at most 64 MiB of HBM per device.

v0:
```python
import functools
import math

import jax
import jax.numpy as jnp
from jax import lax
from jax.experimental import pallas as pl
from jax.experimental.pallas import tpu as pltpu
from jax.sharding import PartitionSpec as P


def from_behind(value, axis, steps):
    count = lax.axis_size(axis)
    leading, last = (max(0, -steps), min(count, count - steps))
    return lax.ppermute(value, axis, [(source, source + steps) for source in range(leading, last)])


def split_parts(values):
    high = values.astype(jnp.bfloat16)
    low = (values - high.astype(jnp.float32)).astype(jnp.bfloat16)
    return (high, low)


def product_two(table, data_bf):
    return jnp.dot(table[0], data_bf, preferred_element_type=jnp.float32) + jnp.dot(
        table[1], data_bf, preferred_element_type=jnp.float32
    )


def product_three(table, data_f32):
    data_high, data_low = split_parts(data_f32)
    total = jnp.dot(table[0], data_high, preferred_element_type=jnp.float32)
    total = total + jnp.dot(table[1], data_high, preferred_element_type=jnp.float32)
    return total + jnp.dot(table[0], data_low, preferred_element_type=jnp.float32)


def correlate(lesser_x, greater_x):
    energies = lesser_x.shape[0]
    length = 2 * energies
    tail_shape = lesser_x.shape[1:]

    def flatten(values, part):
        return values[:, :, part].reshape(energies, -1)

    lesser_re = flatten(lesser_x, 0)
    lesser_im = flatten(lesser_x, 1)
    greater_re = flatten(greater_x, 0)
    greater_im = flatten(greater_x, 1)
    freqs = lax.broadcasted_iota(jnp.int32, (length, energies), 0)
    places = lax.broadcasted_iota(jnp.int32, (length, energies), 1)
    angles = 2.0 * math.pi / length * jnp.mod(freqs * places, length).astype(jnp.float32)
    cosine = split_parts(jnp.cos(angles))
    sine = split_parts(jnp.sin(angles))
    cosine_t = split_parts(jnp.cos(angles).T)
    sine_t = split_parts(jnp.sin(angles).T)
    hat_lre = product_two(cosine, lesser_re) + product_two(sine, lesser_im)
    hat_lim = product_two(cosine, lesser_im) - product_two(sine, lesser_re)
    hat_gre = product_two(cosine, greater_re) - product_two(sine, greater_im)
    hat_gim = product_two(cosine, greater_im) + product_two(sine, greater_re)
    prod_re = hat_lre * hat_gre - hat_lim * hat_gim
    prod_im = hat_lre * hat_gim + hat_lim * hat_gre
    corr_re = (product_three(cosine_t, prod_re) - product_three(sine_t, prod_im)) / length
    corr_im = (product_three(cosine_t, prod_im) + product_three(sine_t, prod_re)) / length
    factor = jnp.float32(energies) ** (-0.5)
    shaped = (energies, tail_shape[0], tail_shape[2], tail_shape[3])
    real_part = (corr_im * factor).reshape(shaped)
    imag_part = (-corr_re * factor).reshape(shaped)
    return jnp.stack([real_part, imag_part], axis=2).astype(jnp.bfloat16)


def left_plain(coupler, blocks):
    return jnp.einsum("ab,ecbd->ecad", coupler, blocks, preferred_element_type=jnp.float32).astype(
        jnp.bfloat16
    )


def left_transposed(coupler, blocks):
    return jnp.einsum("ba,ecbd->ecad", coupler, blocks, preferred_element_type=jnp.float32).astype(
        jnp.bfloat16
    )


def right_transposed(left, coupler):
    return jnp.einsum("ecad,fd->ecaf", left, coupler, preferred_element_type=jnp.float32)


def right_plain(left, coupler):
    return jnp.einsum("ecad,df->ecaf", left, coupler, preferred_element_type=jnp.float32)


def per_device(lesser, greater, coulomb_diag, coulomb_upper):
    greater_t = jnp.swapaxes(greater, 3, 4)
    lesser_x, greater_x = (
        lax.all_to_all(lesser, "energy", split_axis=3, concat_axis=0, tiled=True),
        lax.all_to_all(greater_t, "energy", split_axis=3, concat_axis=0, tiled=True),
    )
    polar_x = correlate(lesser_x, greater_x)
    polar = lax.all_to_all(polar_x, "energy", split_axis=0, concat_axis=3, tiled=True)
    own = polar[:, 0]
    diag_block = coulomb_diag[0]
    upper_block = coulomb_upper[0]
    total = right_transposed(left_plain(diag_block, own), diag_block)
    polar_next = from_behind(polar, "space", -1)
    outgoing = right_plain(left_transposed(upper_block, own), upper_block)
    total = total + right_transposed(left_plain(upper_block, polar_next[:, 0]), upper_block)
    incoming = from_behind(outgoing.astype(jnp.bfloat16), "space", 1).astype(outgoing.dtype)
    total = total + incoming
    return total.astype(jnp.bfloat16)[:, None]


LAGS = 8
STEPS = 4
LANES = 128
MESH = pl.DeviceIdType.MESH


def to_energy(dest):
    return {"energy": dest}


def widen_into(held, at, re, im):
    re, im = re.astype(jnp.float32), im.astype(jnp.float32)
    held[0, at] = re
    held[1, at] = im
    held[2, at] = re + im


def correlate_into(cf, lf, hf, bounds):
    energies, _, rows, _ = cf.shape
    factor = float(energies) ** -0.5

    def one_slab(slab, carry):
        at = pl.ds(pl.multiple_of(slab * 8, 8), 8)
        for first in range(0, energies, LAGS):
            def step(turn, sums):
                start = turn * STEPS
                sums = list(sums)
                for q in range(3):
                    window = [lf[q, start + (first + t), at, :] for t in range(LAGS + STEPS - 1)]
                    taps = [hf[q, start + u, at, :] for u in range(STEPS)]
                    for u in range(STEPS):
                        for j in range(LAGS):
                            sums[q * LAGS + j] = sums[q * LAGS + j] + window[j + u] * taps[u]
                return tuple(sums)

            zero = jnp.zeros((8, LANES), jnp.float32)
            low, high = bounds(first)
            sums = lax.fori_loop(low, high, step, (zero,) * (3 * LAGS))
            for j in range(LAGS):
                rr, ii, mixed = sums[j], sums[LAGS + j], sums[2 * LAGS + j]
                cf[first + j, 0, at, :] = (mixed - rr - ii) * factor
                cf[first + j, 1, at, :] = (ii - rr) * factor
        return carry

    lax.fori_loop(0, rows // 8, one_slab, 0)


def kernel(
    n, ns, lesser, greater, diag_hbm, upper_hbm, out,
    diag, upper, gv, ht, lx, hx, lf, hf, cf, cx, polar, side, uprev, wside, total,
    lxb, hxb, lfb, hfb, cxb, partial,
    local_sem, send_sem, recv_l, recv_h, recv_p, side_send, side_recv, u_send, u_recv, half_send, half_recv,
):
    me = lax.axis_index("energy")
    row = lax.axis_index("space")
    chunks, _, k, _, rows, _ = lx.shape
    energies = n * k
    has_next = row < ns - 1
    has_prev = row > 0
    peers = n // 2
    half, member = me // peers, lax.rem(me, peers)
    own_energies = peers * k
    bands = lxb.shape[0]
    brows = bands * rows
    upper_half, lower_half = half == 1, half == 0

    barrier = pltpu.get_barrier_semaphore()

    def greet(step, carry):
        pl.semaphore_signal(
            barrier, inc=1, device_id=to_energy(lax.rem(me + step, n)), device_id_type=MESH
        )
        return carry

    lax.fori_loop(1, n, greet, 0)

    @pl.when(has_next)
    def _():
        pl.semaphore_signal(barrier, inc=1, device_id={"space": row + 1}, device_id_type=MESH)

    @pl.when(has_prev)
    def _():
        pl.semaphore_signal(barrier, inc=1, device_id={"space": row - 1}, device_id_type=MESH)

    load = pltpu.make_async_copy(greater.at[:, 0], gv, local_sem.at[0])
    load.start()
    load_upper = pltpu.make_async_copy(upper_hbm, upper, local_sem.at[1])
    load_upper.start()
    load_diag = pltpu.make_async_copy(diag_hbm, diag, local_sem.at[2])
    load_diag.start()
    load.wait()
    for e in range(k):
        for part_at in range(2):
            ht[e, part_at] = gv[e, part_at].T

    zeros = jnp.zeros((lf.shape[1] - energies,) + lf.shape[2:], jnp.float32)
    for q in range(3):
        lf[q, pl.ds(energies, lf.shape[1] - energies)] = zeros
    lfb[...] = jnp.zeros(lfb.shape, jnp.float32)

    pl.semaphore_wait(
        barrier, n - 1 + has_next.astype(jnp.int32) + has_prev.astype(jnp.int32)
    )

    def scatter(source, held, c, kind, recv):
        cols = pl.ds(c * LANES, LANES)

        def part(dest):
            return source.at[:, :, pl.ds(pl.multiple_of(dest * rows, rows), rows), cols]

        def push(step, carry):
            dest = lax.rem(me + step, n)
            pltpu.make_async_remote_copy(
                src_ref=part(dest), dst_ref=held.at[c, me], send_sem=send_sem.at[kind],
                recv_sem=recv.at[c], device_id=to_energy(dest), device_id_type=MESH,
            ).start()
            return carry

        lax.fori_loop(1, n, push, 0)
        pltpu.make_async_copy(part(me), held.at[c, me], recv.at[c]).start()

    u_copy = pltpu.make_async_remote_copy(
        src_ref=upper_hbm.at[0], dst_ref=uprev, send_sem=u_send, recv_sem=u_recv,
        device_id={"space": lax.rem(row + 1, ns)}, device_id_type=MESH,
    )

    @pl.when(has_next)
    def _():
        u_copy.start()

    def spread(pick, land, at_half, begin, kind, turn):
        def push(step, carry):
            peer = lax.rem(member + step, peers)
            dest = at_half * peers + peer
            pltpu.make_async_remote_copy(
                src_ref=pick(dest, peer), dst_ref=land(me, member), send_sem=half_send.at[kind],
                recv_sem=half_recv.at[kind, turn], device_id=to_energy(dest), device_id_type=MESH,
            ).start()
            return carry

        lax.fori_loop(begin, peers, push, 0)
        if begin:
            pltpu.make_async_copy(pick(me, member), land(me, member), half_recv.at[kind, turn]).start()

    def band_rows(peer, j):
        return pl.ds(pl.multiple_of(peer * brows + j * rows, rows), rows)

    def band(source, j):
        return lambda dest, peer: source.at[:, :, band_rows(peer, j), pl.ds(0, LANES)]

    def slot(buffer, j):
        return lambda at, peer: buffer.at[j, at]

    @pl.when(lower_half)
    def _():
        for j in range(bands):
            spread(band(ht, j), slot(hxb, j), 1, 0, 2, j)

    @pl.when(upper_half)
    def _():
        for j in range(bands):
            spread(band(lesser.at[:, 0], j), slot(lxb, j), half, 1, 0, j)
            spread(band(ht, j), slot(hxb, j), half, 1, 1, j)
    for c in range(1, chunks):
        scatter(lesser.at[:, 0], lx, c, 0, recv_l)
        scatter(ht, hx, c, 1, recv_h)

    @pl.when(lower_half)
    def _():
        for j in range(bands):
            spread(band(lesser.at[:, 0], j), slot(lxb, j), half, 1, 0, j)
            spread(band(ht, j), slot(hxb, j), half, 1, 1, j)

    load_upper.wait()
    load_diag.wait()
    wside[0] = upper[0]

    @pl.when(has_prev)
    def _():
        u_copy.wait_recv()
        wside[1] = uprev[...].T

    def arrived(buffer, kind, turn):
        pltpu.make_async_copy(buffer, buffer, half_recv.at[kind, turn]).wait()

    some = pl.ds(0, peers)
    own = pl.ds(half * peers, peers)
    short = (own_energies, rows, LANES)

    def half_bounds(first):
        begin = max(0, (own_energies - first - (LAGS + STEPS - 2)) // STEPS)
        low_end, high_end = max(0, own_energies - first) // STEPS, (energies - first) // STEPS
        return half * begin, low_end + half * (high_end - low_end)

    def landing(buffer, j):
        return lambda at, peer: buffer.at[:, :, band_rows(peer, j), :]

    for j in range(bands):
        own_at = pl.ds(half * own_energies, own_energies)
        arrived(lxb.at[j, some], 0, j)
        widen_into(lfb, own_at, lxb[j, own, :, 0].reshape(short), lxb[j, own, :, 1].reshape(short))
        arrived(hxb.at[j, some], 1, j)
        widen_into(hfb, own_at, hxb[j, own, :, 0].reshape(short), hxb[j, own, :, 1].reshape(short))

        @pl.when(upper_half)
        def _():
            arrived(hxb.at[j, some], 2, j)
            re, im = hxb[j, some, :, 0].reshape(short), hxb[j, some, :, 1].reshape(short)
            widen_into(hfb, pl.ds(0, own_energies), re, im)

        correlate_into(cf, lfb, hfb, half_bounds)
        cxb[j] = cf[...].astype(jnp.bfloat16).reshape(cxb.shape[1:])

        @pl.when(upper_half)
        def _():
            spread(lambda dest, peer: cxb.at[j, dest], landing(partial, j), 0, 0, 4, 0)

        spread(lambda dest, peer: cxb.at[j, dest], landing(polar.at[0], j), half, 1, 3, 0)

    def one_chunk(c, carry):
        pltpu.make_async_copy(lx.at[c], lx.at[c], recv_l.at[c]).wait()
        pltpu.make_async_copy(hx.at[c], hx.at[c], recv_h.at[c]).wait()
        flat = (energies, rows, LANES)
        for held, wide in ((lx, lf), (hx, hf)):
            widen_into(wide, pl.ds(0, energies), held[c, :, :, 0].reshape(flat), held[c, :, :, 1].reshape(flat))
        correlate_into(cf, lf, hf, lambda first: (0, (energies - first) // STEPS))
        cx[c] = cf[...].astype(jnp.bfloat16).reshape(cx.shape[1:])
        mine = pl.ds(pl.multiple_of(me * rows, rows), rows)

        def push(step, carry_in):
            dest = lax.rem(me + step, n)
            pltpu.make_async_remote_copy(
                src_ref=cx.at[c, dest], dst_ref=polar.at[c, :, :, mine, :],
                send_sem=send_sem.at[2], recv_sem=recv_p.at[c],
                device_id=to_energy(dest), device_id_type=MESH,
            ).start()
            return carry_in

        lax.fori_loop(1, n, push, 0)
        pltpu.make_async_copy(cx.at[c, me], polar.at[c, :, :, mine, :], recv_p.at[c]).start()
        return carry

    lax.fori_loop(1, chunks, one_chunk, 0)

    def screen(block, coupler, slot, c, begin):
        right = coupler[:, c * LANES:(c + 1) * LANES]
        for e in range(k):
            pair = jnp.concatenate([block[slot, e, 0], block[slot, e, 1]], axis=1)
            left = jnp.dot(coupler, pair, preferred_element_type=jnp.float32).astype(jnp.bfloat16)
            for part_at in range(2):
                term = lax.dot_general(
                    left[:, part_at * LANES:(part_at + 1) * LANES], right,
                    (((1,), (1,)), ((), ())), preferred_element_type=jnp.float32,
                )
                if begin:
                    total[e, part_at] = term
                else:
                    total[e, part_at] += term

    def forward(c, slot, to):
        return pltpu.make_async_remote_copy(
            src_ref=polar.at[c], dst_ref=side.at[slot, c], send_sem=side_send.at[slot, c],
            recv_sem=side_recv.at[slot, c], device_id={"space": to}, device_id_type=MESH,
        )

    up, down = lax.rem(row + 1, ns), lax.rem(row + ns - 1, ns)
    for c in range(chunks):
        if c:
            pltpu.make_async_copy(polar.at[c], polar.at[c], recv_p.at[c]).wait()
        else:
            arrived(polar.at[0], 3, 0)

            @pl.when(lower_half)
            def _():
                arrived(partial, 4, 0)
                both = polar[0].astype(jnp.float32) + partial[...].astype(jnp.float32)
                polar[0] = both.astype(jnp.bfloat16)

        @pl.when(has_prev)
        def _():
            forward(c, 0, down).start()

        @pl.when(has_next)
        def _():
            forward(c, 1, up).start()

        screen(polar, diag[0], c, c, c == 0)

        @pl.when(has_next)
        def _():
            forward(c, 0, down).wait_recv()
            screen(side.at[0], wside[0], c, c, False)

        @pl.when(has_prev)
        def _():
            forward(c, 1, up).wait_recv()
            screen(side.at[1], wside[1], c, c, False)

    out[:, 0] = total[...].astype(jnp.bfloat16)

    for c in range(chunks):
        @pl.when(has_prev)
        def _():
            forward(c, 0, down).wait_send()

        @pl.when(has_next)
        def _():
            forward(c, 1, up).wait_send()

    @pl.when(has_next)
    def _():
        u_copy.wait_send()

    for kind in range(3):
        sent = lx.at[pl.ds(1, chunks - 1), pl.ds(0, n - 1)]
        pltpu.make_async_copy(sent, sent, send_sem.at[kind]).wait()

    def left_here(count, kind):
        sent = lxb.at[:, pl.ds(0, count)]
        pltpu.make_async_copy(sent, sent, half_send.at[kind]).wait()

    for kind in (0, 1, 3):
        left_here(peers - 1, kind)

    @pl.when(lower_half)
    def _():
        left_here(peers, 2)

    @pl.when(upper_half)
    def _():
        left_here(peers, 4)


def fused(n, ns, lesser, greater, diag, upper):
    k, _, _, size, _ = lesser.shape
    rows, chunks, energies = size // n, size // LANES, n * k
    bf, f32 = jnp.bfloat16, jnp.float32
    whole = (k, 2, size, size)
    padded = energies + LAGS + STEPS
    dma = pltpu.SemaphoreType.DMA
    vmem = pl.BlockSpec(memory_space=pltpu.VMEM)
    hbm = pl.BlockSpec(memory_space=pltpu.HBM)
    return pl.pallas_call(
        functools.partial(kernel, n, ns),
        out_shape=jax.ShapeDtypeStruct(lesser.shape, bf),
        in_specs=[hbm] * 4,
        out_specs=vmem,
        scratch_shapes=[
            pltpu.VMEM(diag.shape, bf),
            pltpu.VMEM(upper.shape, bf),
            pltpu.VMEM(whole, bf),
            pltpu.VMEM(whole, bf),
            pltpu.VMEM((chunks, n, k, 2, rows, LANES), bf),
            pltpu.VMEM((chunks, n, k, 2, rows, LANES), bf),
            pltpu.VMEM((3, padded, rows, LANES), f32),
            pltpu.VMEM((3, energies, rows, LANES), f32),
            pltpu.VMEM((energies, 2, rows, LANES), f32),
            pltpu.VMEM((chunks, n, k, 2, rows, LANES), bf),
            pltpu.VMEM((chunks, k, 2, size, LANES), bf),
            pltpu.VMEM((2, chunks, k, 2, size, LANES), bf),
            pltpu.VMEM((size, size), bf),
            pltpu.VMEM((2, size, size), bf),
            pltpu.VMEM(whole, f32),
            pltpu.VMEM((2, n, k, 2, rows, LANES), bf),
            pltpu.VMEM((2, n, k, 2, rows, LANES), bf),
            pltpu.VMEM((3, padded, rows, LANES), f32),
            pltpu.VMEM((3, energies, rows, LANES), f32),
            pltpu.VMEM((2, n, k, 2, rows, LANES), bf),
            pltpu.VMEM((k, 2, size, LANES), bf),
            dma((3,)), dma((3,)), dma((chunks,)), dma((chunks,)), dma((chunks,)),
            dma((2, chunks)), dma((2, chunks)), dma, dma,
            dma((5,)), dma((5, 2)),
        ],
        compiler_params=pltpu.CompilerParams(
            collective_id=0, has_side_effects=True, vmem_limit_bytes=40 << 20
        ),
    )(*(pltpu.with_memory_space_constraint(x, pltpu.HBM) for x in (lesser, greater, diag, upper)))


def fits(n, ns, size, energies):
    banded = n % 2 == 0 and size % n == 0 and (size // n) % 16 == 0 and size % LANES == 0
    return banded and size > LANES and energies % (2 * LAGS) == 0 and ns > 1


def either(n, ns, lesser, greater, diag, upper):
    if fits(n, ns, lesser.shape[3], n * lesser.shape[0]):
        return fused(n, ns, lesser, greater, diag, upper)
    return per_device(lesser, greater, diag, upper)


def solution(mesh):
    placed = (
        P("energy", "space", None, None, None),
        P("energy", "space", None, None, None),
        P("space", None, None),
        P("space", None, None),
    )
    return jax.shard_map(
        functools.partial(either, mesh.shape["energy"], mesh.shape["space"]),
        mesh=mesh,
        in_specs=placed,
        out_specs=P("energy", "space", None, None, None),
        check_vma=False,
    )
```

profile of v0, /device:TPU:1, one launch (start us, length us, event | category | flops | bytes accessed | tf_op | source)
XLA Modules:
  0.0 41.1 jit_solution(3784684764058545802)
XLA Ops:
  0.0 40.2 %shard_map.46 = bf16[2,1,2,256,256]{4,3,2,1,0:T(8,128)(2,1)S(1)} custom-call(bf16[2,1,2,256,256]{4,3,2,1,0:T(8,128)(2,1)} %lesser.1, bf16[2,1,2,256,256]{4,3,2,1,0:T(8,128)(2,1)} %greater.1, bf16[1,256,256]{2,1,0:T(8,128)(2,1)} %diag_hbm.1, bf16[1,256,256]{2,1,0:T(8,128)(2,1)} %upper_hbm.1), custom_call_target="tpu_custom_call" | custom-call | tf_op jit(solution)/shard_map/pallas_call | solution.py:453
  40.3 0.8 %copy.6 = bf16[2,1,2,256,256]{4,3,2,1,0:T(8,128)(2,1)} copy(bf16[2,1,2,256,256]{4,3,2,1,0:T(8,128)(2,1)S(1)} %shard_map.46) | data formatting | bytes 1048576
where the time goes:
time: 41.2 us; the launch traced here: 41.1 us
  Pallas kernels  40.2 us (98%)
  local copies, waits for them, and re-layouts  0.8 us (2%)
    pallas_call x1, Pallas kernels, fused(): pl.pallas_call(functools.partial(kernel, n, ns), out_shape=jax.ShapeDtype...  40.2 us

commit v1 on v0

v1 whole, which is shorter than its diff:
```python
import functools
import math

import jax
import jax.numpy as jnp
from jax import lax
from jax.experimental import pallas as pl
from jax.experimental.pallas import tpu as pltpu
from jax.sharding import PartitionSpec as P


def from_behind(value, axis, steps):
    count = lax.axis_size(axis)
    leading, last = (max(0, -steps), min(count, count - steps))
    return lax.ppermute(value, axis, [(source, source + steps) for source in range(leading, last)])


def split_parts(values):
    high = values.astype(jnp.bfloat16)
    low = (values - high.astype(jnp.float32)).astype(jnp.bfloat16)
    return (high, low)


def product_two(table, data_bf):
    return jnp.dot(table[0], data_bf, preferred_element_type=jnp.float32) + jnp.dot(
        table[1], data_bf, preferred_element_type=jnp.float32
    )


def product_three(table, data_f32):
    data_high, data_low = split_parts(data_f32)
    total = jnp.dot(table[0], data_high, preferred_element_type=jnp.float32)
    total = total + jnp.dot(table[1], data_high, preferred_element_type=jnp.float32)
    return total + jnp.dot(table[0], data_low, preferred_element_type=jnp.float32)


def correlate(lesser_x, greater_x):
    energies = lesser_x.shape[0]
    length = 2 * energies
    tail_shape = lesser_x.shape[1:]

    def flatten(values, part):
        return values[:, :, part].reshape(energies, -1)

    lesser_re = flatten(lesser_x, 0)
    lesser_im = flatten(lesser_x, 1)
    greater_re = flatten(greater_x, 0)
    greater_im = flatten(greater_x, 1)
    freqs = lax.broadcasted_iota(jnp.int32, (length, energies), 0)
    places = lax.broadcasted_iota(jnp.int32, (length, energies), 1)
    angles = 2.0 * math.pi / length * jnp.mod(freqs * places, length).astype(jnp.float32)
    cosine = split_parts(jnp.cos(angles))
    sine = split_parts(jnp.sin(angles))
    cosine_t = split_parts(jnp.cos(angles).T)
    sine_t = split_parts(jnp.sin(angles).T)
    hat_lre = product_two(cosine, lesser_re) + product_two(sine, lesser_im)
    hat_lim = product_two(cosine, lesser_im) - product_two(sine, lesser_re)
    hat_gre = product_two(cosine, greater_re) - product_two(sine, greater_im)
    hat_gim = product_two(cosine, greater_im) + product_two(sine, greater_re)
    prod_re = hat_lre * hat_gre - hat_lim * hat_gim
    prod_im = hat_lre * hat_gim + hat_lim * hat_gre
    corr_re = (product_three(cosine_t, prod_re) - product_three(sine_t, prod_im)) / length
    corr_im = (product_three(cosine_t, prod_im) + product_three(sine_t, prod_re)) / length
    factor = jnp.float32(energies) ** (-0.5)
    shaped = (energies, tail_shape[0], tail_shape[2], tail_shape[3])
    real_part = (corr_im * factor).reshape(shaped)
    imag_part = (-corr_re * factor).reshape(shaped)
    return jnp.stack([real_part, imag_part], axis=2).astype(jnp.bfloat16)


def left_plain(coupler, blocks):
    return jnp.einsum("ab,ecbd->ecad", coupler, blocks, preferred_element_type=jnp.float32).astype(
        jnp.bfloat16
    )


def left_transposed(coupler, blocks):
    return jnp.einsum("ba,ecbd->ecad", coupler, blocks, preferred_element_type=jnp.float32).astype(
        jnp.bfloat16
    )


def right_transposed(left, coupler):
    return jnp.einsum("ecad,fd->ecaf", left, coupler, preferred_element_type=jnp.float32)


def right_plain(left, coupler):
    return jnp.einsum("ecad,df->ecaf", left, coupler, preferred_element_type=jnp.float32)


def per_device(lesser, greater, coulomb_diag, coulomb_upper):
    greater_t = jnp.swapaxes(greater, 3, 4)
    lesser_x, greater_x = (
        lax.all_to_all(lesser, "energy", split_axis=3, concat_axis=0, tiled=True),
        lax.all_to_all(greater_t, "energy", split_axis=3, concat_axis=0, tiled=True),
    )
    polar_x = correlate(lesser_x, greater_x)
    polar = lax.all_to_all(polar_x, "energy", split_axis=0, concat_axis=3, tiled=True)
    own = polar[:, 0]
    diag_block = coulomb_diag[0]
    upper_block = coulomb_upper[0]
    total = right_transposed(left_plain(diag_block, own), diag_block)
    polar_next = from_behind(polar, "space", -1)
    outgoing = right_plain(left_transposed(upper_block, own), upper_block)
    total = total + right_transposed(left_plain(upper_block, polar_next[:, 0]), upper_block)
    incoming = from_behind(outgoing.astype(jnp.bfloat16), "space", 1).astype(outgoing.dtype)
    total = total + incoming
    return total.astype(jnp.bfloat16)[:, None]


GROUPS = 4
LAGS = 8
STEPS = 8
TILE = 16
LANES = 128
FILLER = 0
AHEAD = 2
BEHIND = 2
MESH = pl.DeviceIdType.MESH


def to_energy(dest):
    return {"energy": dest}


def to_space(dest):
    return {"space": dest}


def widen_into(held, block, values):
    count = values.shape[0]
    at = pl.ds(block * count, count)
    re, im = values[:, 0].astype(jnp.float32), values[:, 1].astype(jnp.float32)
    held[0, at] = re
    held[1, at] = im
    held[2, at] = re + im


def correlate_into(target, lf, hf, lag_block, size, begin, end):
    energies, rows = hf.shape[1], hf.shape[2]
    factor = float(energies) ** -0.5

    def one_slab(slab, carry):
        at = pl.ds(pl.multiple_of(slab * 8, 8), 8)
        for first in range(lag_block * size, (lag_block + 1) * size, LAGS):
            def step(turn, sums):
                start = turn * STEPS
                sums = list(sums)
                for q in range(3):
                    window = [lf[q, start + (first + t), at, :] for t in range(LAGS + STEPS - 1)]
                    taps = [hf[q, start + u, at, :] for u in range(STEPS)]
                    for u in range(STEPS):
                        for j in range(LAGS):
                            sums[q * LAGS + j] = sums[q * LAGS + j] + window[j + u] * taps[u]
                return tuple(sums)

            zero = jnp.zeros((8, LANES), jnp.float32)
            low = max(0, begin * size - first - (LAGS - 1)) // STEPS
            high = max(0, end * size - first) // STEPS
            sums = lax.fori_loop(low, high, step, (zero,) * (3 * LAGS))
            for j in range(LAGS):
                rr, ii, mixed = sums[j], sums[LAGS + j], sums[2 * LAGS + j]
                lag = first - lag_block * size + j
                target[lag, 0, at, :] = (mixed - rr - ii) * factor
                target[lag, 1, at, :] = (ii - rr) * factor
        return carry

    lax.fori_loop(0, rows // 8, one_slab, 0)


def kernel(
    n, ns, lesser, greater, diag_hbm, upper_hbm, out,
    diag, upper, lv, gv, ht, held, lf, hf, lff, cf, own_sum, cs, cin, polar, side, uprev, wside, total,
    local_sem, deal_send, deal_recv, z_send, z_recv, c_send, c_recv, back_send, back_recv,
    side_send, side_recv, u_send, u_recv, far,
):
    me = lax.axis_index("energy")
    row = lax.axis_index("space")
    pieces, _, groups, block, _, _, _ = held.shape
    chunks, k, _, size, _ = polar.shape
    members = n // groups
    share = size // members
    stacks = share // TILE
    plane, member = me // members, lax.rem(me, members)
    has_next = row < ns - 1
    has_prev = row > 0
    rest = [p for p in range(pieces) if p != FILLER]

    def column(level):
        return to_energy(level * members + member)

    barrier = pltpu.get_barrier_semaphore()

    def greet(step, carry):
        peer = plane * members + lax.rem(member + step, members)
        pl.semaphore_signal(barrier, inc=1, device_id=to_energy(peer), device_id_type=MESH)
        return carry

    lax.fori_loop(1, members, greet, 0)

    greeted = {0: (1,), 1: (0, 2, 3), 2: (1, 3), 3: ()}
    for level, others in greeted.items():
        if others:
            @pl.when(plane == level)
            def _():
                for other in others:
                    pl.semaphore_signal(barrier, inc=1, device_id=column(other), device_id_type=MESH)

    @pl.when(has_next)
    def _():
        pl.semaphore_signal(barrier, inc=1, device_id=to_space(row + 1), device_id_type=MESH)

    @pl.when(has_prev)
    def _():
        pl.semaphore_signal(barrier, inc=1, device_id=to_space(row - 1), device_id_type=MESH)

    load_g = pltpu.make_async_copy(greater.at[:, 0], gv, local_sem.at[0])
    load_g.start()
    load_l = pltpu.make_async_copy(lesser.at[:, 0], lv, local_sem.at[1])
    load_l.start()
    load_upper = pltpu.make_async_copy(upper_hbm, upper, local_sem.at[2])
    load_upper.start()
    load_diag = pltpu.make_async_copy(diag_hbm, diag, local_sem.at[3])
    load_diag.start()
    load_g.wait()
    for e in range(k):
        for part_at in range(2):
            ht[e, part_at] = gv[e, part_at].T
    lf[...] = jnp.zeros(lf.shape, jnp.float32)
    lff[...] = jnp.zeros(lff.shape, jnp.float32)
    load_l.wait()
    load_upper.wait()
    load_diag.wait()

    two = jnp.logical_or(plane == 1, plane == 3).astype(jnp.int32)
    pl.semaphore_wait(
        barrier, members + two + has_next.astype(jnp.int32) + has_prev.astype(jnp.int32)
    )

    @pl.when(plane == 1)
    def _():
        pl.semaphore_signal(far, inc=1, device_id=column(0), device_id_type=MESH)

    u_copy = pltpu.make_async_remote_copy(
        src_ref=upper_hbm.at[0], dst_ref=uprev, send_sem=u_send, recv_sem=u_recv,
        device_id=to_space(lax.rem(row + 1, ns)), device_id_type=MESH,
    )

    def share_rows(who, p):
        return pl.ds(pl.multiple_of(who * share + (p % stacks) * TILE, TILE), TILE)

    def energies_of(who):
        return pl.ds(pl.multiple_of(who * k, k), k)

    def deal(p, kind):
        source = (lv, ht)[kind]
        cols = pl.ds((p // stacks) * LANES, LANES)
        landing = held.at[p, kind, plane, energies_of(member)]

        def push(step, carry):
            peer = lax.rem(member + step, members)
            pltpu.make_async_remote_copy(
                src_ref=source.at[:, :, share_rows(peer, p), cols], dst_ref=landing,
                send_sem=deal_send.at[kind], recv_sem=deal_recv.at[kind, p],
                device_id=to_energy(plane * members + peer), device_id_type=MESH,
            ).start()
            return carry

        lax.fori_loop(1, members, push, 0)
        pltpu.make_async_copy(
            source.at[:, :, share_rows(member, p), cols], landing, deal_recv.at[kind, p]
        ).start()

    first = rest[0]

    @pl.when(plane < 2)
    def _():
        deal(first, 1)
        deal(FILLER, 1)
        deal(FILLER, 0)
        deal(first, 0)

    @pl.when(plane >= 2)
    def _():
        deal(FILLER, 0)
        deal(FILLER, 1)
        deal(first, 0)
        deal(first, 1)

    for p in rest[1:]:
        deal(p, 1)
        deal(p, 0)

    @pl.when(has_next)
    def _():
        u_copy.start()

    def settle(ref, sem):
        pltpu.make_async_copy(ref, ref, sem).wait()

    def dealt(p, kind, level):
        settle(held.at[p, kind, level], deal_recv.at[kind, p])

    def lift(p, kind, level, to):
        pltpu.make_async_remote_copy(
            src_ref=held.at[p, kind, level], dst_ref=held.at[p, kind, level], send_sem=z_send,
            recv_sem=z_recv.at[p], device_id=column(to), device_id_type=MESH,
        ).start()

    def give(p, lag_block, slot, to):
        pltpu.make_async_remote_copy(
            src_ref=cs.at[p, lag_block], dst_ref=cin.at[p, slot], send_sem=c_send.at[int(p == FILLER)],
            recv_sem=c_recv.at[p], device_id=column(to), device_id_type=MESH,
        ).start()

    def back(source, p):
        c = p // stacks
        landing = polar.at[c, :, :, share_rows(member, p), :]

        def push(step, carry):
            peer = lax.rem(member + step, members)
            pltpu.make_async_remote_copy(
                src_ref=source.at[energies_of(peer)], dst_ref=landing,
                send_sem=back_send, recv_sem=back_recv.at[c],
                device_id=to_energy(plane * members + peer), device_id_type=MESH,
            ).start()
            return carry

        lax.fori_loop(1, members, push, 0)
        pltpu.make_async_copy(source.at[energies_of(member)], landing, back_recv.at[c]).start()

    def screen(source, coupler, c, begin):
        right = coupler[:, c * LANES:(c + 1) * LANES]
        for e in range(k):
            pair = jnp.concatenate([source[e, 0], source[e, 1]], axis=1)
            left = jnp.dot(coupler, pair, preferred_element_type=jnp.float32).astype(jnp.bfloat16)
            for part_at in range(2):
                term = lax.dot_general(
                    left[:, part_at * LANES:(part_at + 1) * LANES], right,
                    (((1,), (1,)), ((), ())), preferred_element_type=jnp.float32,
                )
                if begin:
                    total[e, part_at] = term
                else:
                    total[e, part_at] += term

    up, down = lax.rem(row + 1, ns), lax.rem(row + ns - 1, ns)

    def forward(c, slot, to):
        return pltpu.make_async_remote_copy(
            src_ref=polar.at[c], dst_ref=side.at[slot, c], send_sem=side_send.at[slot, c],
            recv_sem=side_recv.at[slot, c], device_id=to_space(to), device_id_type=MESH,
        )

    def screen_own(c):
        settle(polar.at[c], back_recv.at[c])

        @pl.when(has_prev)
        def _():
            forward(c, 0, down).start()

        @pl.when(has_next)
        def _():
            forward(c, 1, up).start()

        screen(polar.at[c], diag[0], c, c == 0)

    def screen_sides(c):
        @pl.when(has_next)
        def _():
            forward(c, 0, down).wait_recv()
            screen(side.at[0, c], wside[0], c, False)

        @pl.when(has_prev)
        def _():
            forward(c, 1, up).wait_recv()
            screen(side.at[1, c], wside[1], c, False)

    def ready_couplers():
        wside[0] = upper[0]

        @pl.when(has_prev)
        def _():
            u_copy.wait_recv()
            wside[1] = uprev[...].T

    def middle(turn):
        c = (turn - BEHIND) // stacks - 1
        when = (turn - BEHIND) % stacks
        if 0 <= c < chunks - 1 and when == 1:
            if c == 0:
                ready_couplers()
            screen_own(c)
            screen_sides(c)

    def add(p, lag_block, slots):
        settle(cin.at[p, pl.ds(0, slots)], c_recv.at[p])
        value = own_sum[p]
        for slot in range(slots):
            value = value + cin[p, slot].astype(jnp.float32)
        cs[p, lag_block] = value.astype(jnp.bfloat16)
        back(cs.at[p, lag_block], p)

    def relay(p):
        settle(cin.at[p, 0], c_recv.at[p])
        back(cin.at[p, 0], p)

    turns = range(1, len(rest) + BEHIND + 1)
    meet = BEHIND + 2

    def at_turn(turn):
        return rest[turn - 1] if 1 <= turn <= len(rest) else None

    def rounded(p, lag_block):
        cs[p, lag_block] = cf[...].astype(jnp.bfloat16)

    @pl.when(plane == 0)
    def _():
        def send(p):
            dealt(p, 1, 0)
            if p != FILLER:
                lift(p, 1, 0, 2)
            lift(p, 1, 0, 1)

        pl.semaphore_wait(far, 1)
        send(first)
        send(FILLER)
        dealt(FILLER, 0, 0)
        lift(FILLER, 0, 0, 1)
        for turn in range(2, AHEAD + 1):
            send(at_turn(turn))
        for turn in turns:
            ahead, p, done = at_turn(turn + AHEAD), at_turn(turn), at_turn(turn - BEHIND)
            if ahead is not None:
                send(ahead)
            if p is not None:
                dealt(p, 0, 0)
                widen_into(lf, 0, held[p, 0, 0])
                widen_into(hf, 0, held[p, 1, 0])
                correlate_into(own_sum.at[p], lf, hf, 0, block, 0, 1)
            if turn == meet:
                relay(FILLER)
            if done is not None:
                add(done, 0, 2)
            middle(turn)

    @pl.when(plane == 1)
    def _():
        def send(p):
            dealt(p, 1, 1)
            lift(p, 1, 1, 2)

        for turn in range(1, AHEAD + 1):
            send(at_turn(turn))
        for turn in turns:
            ahead, p, done = at_turn(turn + AHEAD), at_turn(turn), at_turn(turn - BEHIND)
            if ahead is not None:
                send(ahead)
            if p is not None:
                dealt(p, 0, 1)
                widen_into(lf, 1, held[p, 0, 1])
                widen_into(hf, 1, held[p, 1, 1])
                settle(held.at[p, 1, 0], z_recv.at[p])
                widen_into(hf, 0, held[p, 1, 0])
                correlate_into(cf, lf, hf, 0, block, 1, 2)
                rounded(p, 0)
                give(p, 0, 0, 0)
                correlate_into(own_sum.at[p], lf, hf, 1, block, 1, 2)
            if turn == BEHIND:
                dealt(FILLER, 0, 1)
                dealt(FILLER, 1, 1)
                settle(held.at[FILLER, :, pl.ds(0, groups - 1)], z_recv.at[FILLER])
                for level in range(groups):
                    widen_into(lff, level, held[FILLER, 0, level])
                    widen_into(hf, level, held[FILLER, 1, level])
                for lag_block in (0, 2, 3, 1):
                    correlate_into(cf, lff, hf, lag_block, block, 0, groups)
                    rounded(FILLER, lag_block)
                    if lag_block == 1:
                        back(cs.at[FILLER, 1], FILLER)
                    else:
                        give(FILLER, lag_block, 0, lag_block)
            if done is not None:
                add(done, 1, 1)
            middle(turn)

    @pl.when(plane == 2)
    def _():
        dealt(FILLER, 0, 2)
        lift(FILLER, 0, 2, 1)
        dealt(FILLER, 1, 2)
        lift(FILLER, 1, 2, 1)
        for turn in turns:
            p = at_turn(turn)
            if p is not None:
                dealt(p, 0, 2)
                dealt(p, 1, 2)
                widen_into(lf, 2, held[p, 0, 2])
                widen_into(hf, 2, held[p, 1, 2])
                settle(held.at[p, 0, pl.ds(0, groups)], z_recv.at[p])
                widen_into(lf, 3, held[p, 0, 3])
                for level in (0, 1, 3):
                    widen_into(hf, level, held[p, 1, level])
                for lag_block in (0, 1, 3, 2):
                    correlate_into(cf, lf, hf, lag_block, block, 2, groups)
                    rounded(p, lag_block)
                    if lag_block == 2:
                        back(cs.at[p, 2], p)
                    else:
                        give(p, lag_block, 0 if lag_block == 1 or lag_block == 3 else 1, lag_block)
            if turn == meet:
                relay(FILLER)
            middle(turn)

    @pl.when(plane == 3)
    def _():
        def send(p, to):
            for kind in range(2):
                dealt(p, kind, 3)
                lift(p, kind, 3, to)

        send(first, 2)
        send(FILLER, 1)
        for p in rest[1:]:
            send(p, 2)
        for turn in turns:
            p = at_turn(turn)
            if p is not None:
                relay(p)
            if turn == meet:
                relay(FILLER)
            middle(turn)

    last = chunks - 1
    screen_own(last)
    screen_sides(last)
    out[:, 0] = total[...].astype(jnp.bfloat16)

    for c in range(chunks):
        @pl.when(has_prev)
        def _():
            forward(c, 0, down).wait_send()

        @pl.when(has_next)
        def _():
            forward(c, 1, up).wait_send()

    @pl.when(has_next)
    def _():
        u_copy.wait_send()

    for sem in (deal_send.at[0], deal_send.at[1], back_send):
        settle(held.at[:, 0, 0, pl.ds(0, k * (members - 1))], sem)

    others = pl.ds(0, len(rest))

    @pl.when(jnp.logical_or(plane == 0, plane == 3))
    def _():
        settle(held.at[:, 0, pl.ds(0, 2)], z_send)

    @pl.when(plane == 1)
    def _():
        settle(held.at[others, 0, 0], z_send)
        settle(cs.at[others, 0], c_send.at[0])
        settle(cs.at[0, pl.ds(0, 3)], c_send.at[1])

    @pl.when(plane == 2)
    def _():
        settle(held.at[0, 0, pl.ds(0, 2)], z_send)
        settle(cs.at[others, pl.ds(0, 3)], c_send.at[0])


def fused(n, ns, lesser, greater, diag, upper):
    k, _, _, size, _ = lesser.shape
    members, energies, chunks = n // GROUPS, n * k, size // LANES
    block = members * k
    pieces = chunks * (size // members // TILE)
    bf, f32 = jnp.bfloat16, jnp.float32
    whole = (k, 2, size, size)
    piece = (block, 2, TILE, LANES)
    padded = energies + LAGS + STEPS
    dma = pltpu.SemaphoreType.DMA
    vmem = pl.BlockSpec(memory_space=pltpu.VMEM)
    hbm = pl.BlockSpec(memory_space=pltpu.HBM)
    return pl.pallas_call(
        functools.partial(kernel, n, ns),
        out_shape=jax.ShapeDtypeStruct(lesser.shape, bf),
        in_specs=[hbm] * 4,
        out_specs=vmem,
        scratch_shapes=[
            pltpu.VMEM(diag.shape, bf),
            pltpu.VMEM(upper.shape, bf),
            pltpu.VMEM(whole, bf),
            pltpu.VMEM(whole, bf),
            pltpu.VMEM(whole, bf),
            pltpu.VMEM((pieces, 2, GROUPS) + piece, bf),
            pltpu.VMEM((3, padded, TILE, LANES), f32),
            pltpu.VMEM((3, energies, TILE, LANES), f32),
            pltpu.VMEM((3, padded, TILE, LANES), f32),
            pltpu.VMEM(piece, f32),
            pltpu.VMEM((pieces,) + piece, f32),
            pltpu.VMEM((pieces, GROUPS) + piece, bf),
            pltpu.VMEM((pieces, 2) + piece, bf),
            pltpu.VMEM((chunks, k, 2, size, LANES), bf),
            pltpu.VMEM((2, chunks, k, 2, size, LANES), bf),
            pltpu.VMEM((size, size), bf),
            pltpu.VMEM((2, size, size), bf),
            pltpu.VMEM(whole, f32),
            dma((4,)), dma((2,)), dma((2, pieces)), dma, dma((pieces,)), dma((2,)), dma((pieces,)),
            dma, dma((chunks,)), dma((2, chunks)), dma((2, chunks)), dma, dma,
            pltpu.SemaphoreType.REGULAR,
        ],
        compiler_params=pltpu.CompilerParams(
            collective_id=0, has_side_effects=True, vmem_limit_bytes=40 << 20
        ),
    )(*(pltpu.with_memory_space_constraint(x, pltpu.HBM) for x in (lesser, greater, diag, upper)))


def fits(n, ns, size, k):
    if n % GROUPS or size % LANES or size <= LANES or ns < 2:
        return False
    members = n // GROUPS
    if members < 2 or size % (members * TILE) or (members * k) % STEPS:
        return False
    stacks = size // members // TILE
    return 2 <= stacks and size // LANES * stacks <= 16


def either(n, ns, lesser, greater, diag, upper):
    if fits(n, ns, lesser.shape[3], lesser.shape[0]):
        return fused(n, ns, lesser, greater, diag, upper)
    return per_device(lesser, greater, diag, upper)


def solution(mesh):
    placed = (
        P("energy", "space", None, None, None),
        P("energy", "space", None, None, None),
        P("space", None, None),
        P("space", None, None),
    )
    return jax.shard_map(
        functools.partial(either, mesh.shape["energy"], mesh.shape["space"]),
        mesh=mesh,
        in_specs=placed,
        out_specs=P("energy", "space", None, None, None),
        check_vma=False,
    )
```

time: 41.2 us -> 44.3 us (1.075)
  Pallas kernels: 40.2 us -> 43.4 us
    pallas_call x1, Pallas kernels: 40.2 us -> 43.4 us  [fused(): pl.pallas_call(functools.partial(kernel, n, ns), out_shape=jax.ShapeDtype...]
where the time goes in v1:
time: 44.3 us; the launch traced here: 44.2 us
  Pallas kernels  43.4 us (98%)
  local copies, waits for them, and re-layouts  0.8 us (2%)
    pallas_call x1, Pallas kernels, fused(): pl.pallas_call(functools.partial(kernel, n, ns), out_shape=jax.ShapeDtype...  43.4 us

profile of v1, /device:TPU:1, one launch (start us, length us, event | category | flops | bytes accessed | tf_op | source)
XLA Modules:
  0.0 44.2 jit_solution(8431548179762103821)
XLA Ops:
  0.0 43.4 %shard_map.46 = bf16[2,1,2,256,256]{4,3,2,1,0:T(8,128)(2,1)S(1)} custom-call(bf16[2,1,2,256,256]{4,3,2,1,0:T(8,128)(2,1)} %lesser.1, bf16[2,1,2,256,256]{4,3,2,1,0:T(8,128)(2,1)} %greater.1, bf16[1,256,256]{2,1,0:T(8,128)(2,1)} %diag_hbm.1, bf16[1,256,256]{2,1,0:T(8,128)(2,1)} %upper_hbm.1), custom_call_target="tpu_custom_call" | custom-call | tf_op jit(solution)/shard_map/pallas_call | solution.py:585
  43.4 0.8 %copy.6 = bf16[2,1,2,256,256]{4,3,2,1,0:T(8,128)(2,1)} copy(bf16[2,1,2,256,256]{4,3,2,1,0:T(8,128)(2,1)S(1)} %shard_map.46) | data formatting | bytes 1048576

commit v2 on v1

v2 whole, which is shorter than its diff:
```python
import functools
import math

import jax
import jax.numpy as jnp
from jax import lax
from jax.experimental import pallas as pl
from jax.experimental.pallas import tpu as pltpu
from jax.sharding import PartitionSpec as P


def from_behind(value, axis, steps):
    count = lax.axis_size(axis)
    leading, last = (max(0, -steps), min(count, count - steps))
    return lax.ppermute(value, axis, [(source, source + steps) for source in range(leading, last)])


def split_parts(values):
    high = values.astype(jnp.bfloat16)
    low = (values - high.astype(jnp.float32)).astype(jnp.bfloat16)
    return (high, low)


def product_two(table, data_bf):
    return jnp.dot(table[0], data_bf, preferred_element_type=jnp.float32) + jnp.dot(
        table[1], data_bf, preferred_element_type=jnp.float32
    )


def product_three(table, data_f32):
    data_high, data_low = split_parts(data_f32)
    total = jnp.dot(table[0], data_high, preferred_element_type=jnp.float32)
    total = total + jnp.dot(table[1], data_high, preferred_element_type=jnp.float32)
    return total + jnp.dot(table[0], data_low, preferred_element_type=jnp.float32)


def correlate(lesser_x, greater_x):
    energies = lesser_x.shape[0]
    length = 2 * energies
    tail_shape = lesser_x.shape[1:]

    def flatten(values, part):
        return values[:, :, part].reshape(energies, -1)

    lesser_re = flatten(lesser_x, 0)
    lesser_im = flatten(lesser_x, 1)
    greater_re = flatten(greater_x, 0)
    greater_im = flatten(greater_x, 1)
    freqs = lax.broadcasted_iota(jnp.int32, (length, energies), 0)
    places = lax.broadcasted_iota(jnp.int32, (length, energies), 1)
    angles = 2.0 * math.pi / length * jnp.mod(freqs * places, length).astype(jnp.float32)
    cosine = split_parts(jnp.cos(angles))
    sine = split_parts(jnp.sin(angles))
    cosine_t = split_parts(jnp.cos(angles).T)
    sine_t = split_parts(jnp.sin(angles).T)
    hat_lre = product_two(cosine, lesser_re) + product_two(sine, lesser_im)
    hat_lim = product_two(cosine, lesser_im) - product_two(sine, lesser_re)
    hat_gre = product_two(cosine, greater_re) - product_two(sine, greater_im)
    hat_gim = product_two(cosine, greater_im) + product_two(sine, greater_re)
    prod_re = hat_lre * hat_gre - hat_lim * hat_gim
    prod_im = hat_lre * hat_gim + hat_lim * hat_gre
    corr_re = (product_three(cosine_t, prod_re) - product_three(sine_t, prod_im)) / length
    corr_im = (product_three(cosine_t, prod_im) + product_three(sine_t, prod_re)) / length
    factor = jnp.float32(energies) ** (-0.5)
    shaped = (energies, tail_shape[0], tail_shape[2], tail_shape[3])
    real_part = (corr_im * factor).reshape(shaped)
    imag_part = (-corr_re * factor).reshape(shaped)
    return jnp.stack([real_part, imag_part], axis=2).astype(jnp.bfloat16)


def left_plain(coupler, blocks):
    return jnp.einsum("ab,ecbd->ecad", coupler, blocks, preferred_element_type=jnp.float32).astype(
        jnp.bfloat16
    )


def left_transposed(coupler, blocks):
    return jnp.einsum("ba,ecbd->ecad", coupler, blocks, preferred_element_type=jnp.float32).astype(
        jnp.bfloat16
    )


def right_transposed(left, coupler):
    return jnp.einsum("ecad,fd->ecaf", left, coupler, preferred_element_type=jnp.float32)


def right_plain(left, coupler):
    return jnp.einsum("ecad,df->ecaf", left, coupler, preferred_element_type=jnp.float32)


def per_device(lesser, greater, coulomb_diag, coulomb_upper):
    greater_t = jnp.swapaxes(greater, 3, 4)
    lesser_x, greater_x = (
        lax.all_to_all(lesser, "energy", split_axis=3, concat_axis=0, tiled=True),
        lax.all_to_all(greater_t, "energy", split_axis=3, concat_axis=0, tiled=True),
    )
    polar_x = correlate(lesser_x, greater_x)
    polar = lax.all_to_all(polar_x, "energy", split_axis=0, concat_axis=3, tiled=True)
    own = polar[:, 0]
    diag_block = coulomb_diag[0]
    upper_block = coulomb_upper[0]
    total = right_transposed(left_plain(diag_block, own), diag_block)
    polar_next = from_behind(polar, "space", -1)
    outgoing = right_plain(left_transposed(upper_block, own), upper_block)
    total = total + right_transposed(left_plain(upper_block, polar_next[:, 0]), upper_block)
    incoming = from_behind(outgoing.astype(jnp.bfloat16), "space", 1).astype(outgoing.dtype)
    total = total + incoming
    return total.astype(jnp.bfloat16)[:, None]


GROUPS = 4
LAGS = 8
STEPS = 8
TILE = 16
LANES = 128
AHEAD = 4
STRAIGHT = 2
LATE = 1
FIRST = 3
MESH = pl.DeviceIdType.MESH


def to_energy(dest):
    return {"energy": dest}


def to_space(dest):
    return {"space": dest}


def widen_into(held, block, values):
    count = values.shape[0]
    at = pl.ds(block * count, count)
    re, im = values[:, 0].astype(jnp.float32), values[:, 1].astype(jnp.float32)
    held[0, at] = re
    held[1, at] = im
    held[2, at] = re + im


def correlate_into(target, lf, hf, lag_block, size, begin, end):
    energies, rows = hf.shape[1], hf.shape[2]
    factor = float(energies) ** -0.5

    def one_slab(slab, carry):
        at = pl.ds(pl.multiple_of(slab * 8, 8), 8)
        for first in range(lag_block * size, (lag_block + 1) * size, LAGS):
            def step(turn, sums):
                start = turn * STEPS
                sums = list(sums)
                for q in range(3):
                    window = [lf[q, start + (first + t), at, :] for t in range(LAGS + STEPS - 1)]
                    taps = [hf[q, start + u, at, :] for u in range(STEPS)]
                    for u in range(STEPS):
                        for j in range(LAGS):
                            sums[q * LAGS + j] = sums[q * LAGS + j] + window[j + u] * taps[u]
                return tuple(sums)

            zero = jnp.zeros((8, LANES), jnp.float32)
            low = max(0, begin * size - first - (LAGS - 1)) // STEPS
            high = max(0, end * size - first) // STEPS
            sums = lax.fori_loop(low, high, step, (zero,) * (3 * LAGS))
            for j in range(LAGS):
                rr, ii, mixed = sums[j], sums[LAGS + j], sums[2 * LAGS + j]
                lag = first - lag_block * size + j
                target[lag, 0, at, :] = (mixed - rr - ii) * factor
                target[lag, 1, at, :] = (ii - rr) * factor
        return carry

    lax.fori_loop(0, rows // 8, one_slab, 0)


def kernel(
    n, ns, lesser, greater, diag_hbm, upper_hbm, out,
    diag, upper, gv, ht, held, lf, hf, cf, own_sum, cs, cin, late, polar, side, uprev, wside, total,
    local_sem, deal_send, deal_recv, z_send, z_recv, h_recv, c_send, c_recv, late_recv, back_send, back_recv,
    side_send, side_recv, u_send, u_recv,
):
    me = lax.axis_index("energy")
    row = lax.axis_index("space")
    pieces, _, groups, block, _, _, _ = held.shape
    chunks, k, _, size, _ = polar.shape
    members = n // groups
    stack = members * TILE
    stacks = size // stack
    plane, member = me // members, lax.rem(me, members)
    has_next = row < ns - 1
    has_prev = row > 0
    straight_in = range(STRAIGHT)
    straight_out = range(pieces - STRAIGHT, pieces)

    def column(level):
        return to_energy(level * members + member)

    barrier = pltpu.get_barrier_semaphore()

    def greet(step, carry):
        peer = plane * members + lax.rem(member + step, members)
        pl.semaphore_signal(barrier, inc=1, device_id=to_energy(peer), device_id_type=MESH)
        return carry

    lax.fori_loop(1, members, greet, 0)

    @pl.when(plane == 0)
    def _():
        pl.semaphore_signal(barrier, inc=1, device_id=column(2), device_id_type=MESH)

    @pl.when(plane == 1)
    def _():
        pl.semaphore_signal(barrier, inc=1, device_id=column(0), device_id_type=MESH)

    @pl.when(plane == 2)
    def _():
        pl.semaphore_signal(barrier, inc=1, device_id=column(1), device_id_type=MESH)
        for peer in range(members):
            pl.semaphore_signal(barrier, inc=1, device_id=to_energy(3 * members + peer), device_id_type=MESH)

    @pl.when(has_next)
    def _():
        pl.semaphore_signal(barrier, inc=1, device_id=to_space(row + 1), device_id_type=MESH)

    @pl.when(has_prev)
    def _():
        pl.semaphore_signal(barrier, inc=1, device_id=to_space(row - 1), device_id_type=MESH)

    def load(c):
        rows = pl.ds(c * LANES, LANES)
        return pltpu.make_async_copy(greater.at[:, 0, :, rows, :], gv.at[:, :, rows, :], local_sem.at[c])

    for c in range(chunks):
        load(c).start()

    def turn_over(c):
        load(c).wait()
        cols = slice(c * LANES, (c + 1) * LANES)
        for e in range(k):
            for part_at in range(2):
                ht[e, part_at, :, cols] = gv[e, part_at, cols, :].T

    @pl.when(plane < 2)
    def _():
        turn_over(0)

    more_greet = (members - 1) * (plane == 3).astype(jnp.int32)
    pl.semaphore_wait(
        barrier, members + more_greet + has_next.astype(jnp.int32) + has_prev.astype(jnp.int32)
    )

    u_copy = pltpu.make_async_remote_copy(
        src_ref=upper_hbm.at[0], dst_ref=uprev, send_sem=u_send, recv_sem=u_recv,
        device_id=to_space(lax.rem(row + 1, ns)), device_id_type=MESH,
    )

    def tile_of(who):
        return pl.ds(pl.multiple_of(who * TILE, TILE), TILE)

    def share_rows(who, p):
        return pl.ds(pl.multiple_of((p % stacks) * stack + who * TILE, TILE), TILE)

    def piece_rows(p):
        return pl.ds((p % stacks) * stack, stack)

    def energies_of(who):
        return pl.ds(pl.multiple_of(who * k, k), k)

    def part(p, kind, who):
        source = (lesser.at[:, 0], ht)[kind]
        return source.at[:, :, share_rows(who, p), pl.ds((p // stacks) * LANES, LANES)]

    def deal(p, kind):
        landing = held.at[p, kind, plane, energies_of(member)]

        def push(step, carry):
            peer = lax.rem(member + step, members)
            pltpu.make_async_remote_copy(
                src_ref=part(p, kind, peer), dst_ref=landing,
                send_sem=deal_send.at[kind], recv_sem=deal_recv.at[kind, p],
                device_id=to_energy(plane * members + peer), device_id_type=MESH,
            ).start()
            return carry

        lax.fori_loop(1, members, push, 0)
        pltpu.make_async_copy(part(p, kind, member), landing, deal_recv.at[kind, p]).start()

    def drop(p, kind):
        def push(step, carry):
            peer = lax.rem(member + step, members)
            pltpu.make_async_remote_copy(
                src_ref=part(p, kind, peer), dst_ref=held.at[p, kind, 3, energies_of(member)],
                send_sem=z_send, recv_sem=z_recv.at[p],
                device_id=to_energy(2 * members + peer), device_id_type=MESH,
            ).start()
            return carry

        lax.fori_loop(0, members, push, 0)

    lead = min(AHEAD, pieces)

    @pl.when(plane < 2)
    def _():
        for p in range(lead):
            deal(p, 1)

    @pl.when(plane == 2)
    def _():
        deal(0, 0)
        turn_over(0)
        deal(0, 1)

    @pl.when(plane == 3)
    def _():
        drop(0, 0)
        turn_over(0)
        drop(0, 1)

    for c in range(1, chunks):
        turn_over(c)

    @pl.when(plane < 2)
    def _():
        for p in range(pieces):
            deal(p, 0)
            if p + lead < pieces:
                deal(p + lead, 1)

    @pl.when(plane == 2)
    def _():
        for p in range(1, pieces):
            deal(p, 0)
            deal(p, 1)

    @pl.when(plane == 3)
    def _():
        for p in range(1, pieces):
            for kind in range(2):
                if p in straight_in:
                    drop(p, kind)
                else:
                    deal(p, kind)

    load_upper = pltpu.make_async_copy(upper_hbm, upper, local_sem.at[chunks])
    load_upper.start()
    load_diag = pltpu.make_async_copy(diag_hbm, diag, local_sem.at[chunks + 1])
    load_diag.start()
    lf[...] = jnp.zeros(lf.shape, jnp.float32)

    @pl.when(has_next)
    def _():
        u_copy.start()

    def settle(ref, sem):
        pltpu.make_async_copy(ref, ref, sem).wait()

    def dealt(p, kind, level):
        settle(held.at[p, kind, level], deal_recv.at[kind, p])

    def lift(p, kind, level, to, recv):
        pltpu.make_async_remote_copy(
            src_ref=held.at[p, kind, level], dst_ref=held.at[p, kind, level], send_sem=z_send,
            recv_sem=recv.at[p], device_id=column(to), device_id_type=MESH,
        ).start()

    def give(p, lag_block, slot):
        pltpu.make_async_remote_copy(
            src_ref=cs.at[p, lag_block], dst_ref=cin.at[p, slot], send_sem=c_send,
            recv_sem=c_recv.at[p], device_id=column(lag_block), device_id_type=MESH,
        ).start()

    def give_straight(p, lag_block):
        at = p - straight_out[0]

        def push(step, carry):
            peer = lax.rem(member + step, members)
            pltpu.make_async_remote_copy(
                src_ref=cs.at[p, lag_block, energies_of(peer)], dst_ref=late.at[at, :, :, tile_of(member), :],
                send_sem=c_send, recv_sem=late_recv.at[at],
                device_id=to_energy(lag_block * members + peer), device_id_type=MESH,
            ).start()
            return carry

        lax.fori_loop(0, members, push, 0)

    def back(source, p):
        landing = polar.at[p // stacks, :, :, share_rows(member, p), :]

        def push(step, carry):
            peer = lax.rem(member + step, members)
            pltpu.make_async_remote_copy(
                src_ref=source.at[energies_of(peer)], dst_ref=landing,
                send_sem=back_send, recv_sem=back_recv.at[p],
                device_id=to_energy(plane * members + peer), device_id_type=MESH,
            ).start()
            return carry

        lax.fori_loop(1, members, push, 0)
        pltpu.make_async_copy(source.at[energies_of(member)], landing, back_recv.at[p]).start()

    def terms(source, coupler, c):
        right = coupler[:, c * LANES:(c + 1) * LANES]
        for e in range(k):
            pair = jnp.concatenate([source[e, 0], source[e, 1]], axis=1)
            left = jnp.dot(coupler, pair, preferred_element_type=jnp.float32).astype(jnp.bfloat16)
            for part_at in range(2):
                yield e, part_at, lax.dot_general(
                    left[:, part_at * LANES:(part_at + 1) * LANES], right,
                    (((1,), (1,)), ((), ())), preferred_element_type=jnp.float32,
                )

    def screen(source, coupler, c, begin):
        for e, part_at, term in terms(source, coupler, c):
            if begin:
                total[e, part_at] = term
            else:
                total[e, part_at] += term

    def finish(source, coupler, c):
        for e, part_at, term in terms(source, coupler, c):
            out[e, 0, part_at] = (total[e, part_at] + term).astype(jnp.bfloat16)

    up, down = lax.rem(row + 1, ns), lax.rem(row + ns - 1, ns)

    def forward(p, slot, to):
        place = (p // stacks, slice(None), slice(None), piece_rows(p))
        return pltpu.make_async_remote_copy(
            src_ref=polar.at[place], dst_ref=side.at[(slot,) + place], send_sem=side_send.at[slot],
            recv_sem=side_recv.at[slot, p // stacks], device_id=to_space(to), device_id_type=MESH,
        )

    def hand_over(p):
        place = (p // stacks, slice(None), slice(None), piece_rows(p))
        settle(polar.at[place], back_recv.at[p])
        if p in straight_out:
            @pl.when(plane < 2)
            def _():
                at = p - straight_out[0]
                settle(late.at[at], late_recv.at[at])
                both = polar[place].astype(jnp.float32) + late[at].astype(jnp.float32)
                polar[place] = both.astype(jnp.bfloat16)

        @pl.when(has_prev)
        def _():
            forward(p, 0, down).start()

        @pl.when(has_next)
        def _():
            forward(p, 1, up).start()

    def screen_own(c):
        for p in range(c * stacks, (c + 1) * stacks):
            hand_over(p)
        screen(polar.at[c], diag[0], c, c == 0)

    def from_next(c, act):
        @pl.when(has_next)
        def _():
            settle(side.at[0, c], side_recv.at[0, c])
            act(side.at[0, c], wside[0], c)

    def from_prev(c, act):
        @pl.when(has_prev)
        def _():
            settle(side.at[1, c], side_recv.at[1, c])
            act(side.at[1, c], wside[1], c)

    def more(source, coupler, c):
        screen(source, coupler, c, False)

    def screen_sides(c):
        from_next(c, more)
        from_prev(c, more)

    def couplers():
        load_upper.wait()
        load_diag.wait()
        wside[0] = upper[0]

        @pl.when(has_prev)
        def _():
            u_copy.wait_recv()
            wside[1] = uprev[...].T

    def middle(p):
        c = (p - 1) // stacks - 1
        if 0 <= c < chunks - 1 and (p - 1) % stacks == 0:
            if c == 0:
                couplers()
            screen_own(c)

    def add(p, lag_block, slots):
        value = own_sum[p]
        if slots:
            settle(cin.at[p, pl.ds(0, slots)], c_recv.at[p])
        for slot in range(slots):
            value = value + cin[p, slot].astype(jnp.float32)
        cs[p, lag_block] = value.astype(jnp.bfloat16)
        back(cs.at[p, lag_block], p)

    def rounded(p, lag_block):
        cs[p, lag_block] = cf[...].astype(jnp.bfloat16)

    early = list(range(max(0, stacks - 1)))
    order = early + list(straight_out) + [p for p in range(pieces) if p not in early and p not in straight_out]

    @pl.when(plane == 0)
    def _():
        def send(p):
            dealt(p, 1, 0)
            lift(p, 1, 0, 1, h_recv)

        for p in range(pieces):
            send(p)
        for p in range(pieces):
            dealt(p, 0, 0)
            widen_into(lf, 0, held[p, 0, 0])
            widen_into(hf, 0, held[p, 1, 0])
            correlate_into(own_sum.at[p], lf, hf, 0, block, 0, 1)
        for p in order:
            add(p, 0, 1 if p in straight_out else 2)
            middle(p)

    @pl.when(plane == 1)
    def _():
        def send(p):
            dealt(p, 1, 1)
            lift(p, 1, 1, 2, z_recv)

        for p in range(FIRST):
            send(p)
        held_back = []
        for p in range(pieces):
            settle(held.at[p, 1, 0], h_recv.at[p])
            lift(p, 1, 0, 2, h_recv)
            if p + FIRST < pieces:
                send(p + FIRST)
            dealt(p, 0, 1)
            widen_into(lf, 1, held[p, 0, 1])
            widen_into(hf, 1, held[p, 1, 1])
            widen_into(hf, 0, held[p, 1, 0])
            correlate_into(cf, lf, hf, 0, block, 1, 2)
            rounded(p, 0)
            if p in early or p in straight_out:
                give(p, 0, 0)
            else:
                held_back.append(p)
            correlate_into(own_sum.at[p], lf, hf, 1, block, 1, 2)
        for p in held_back:
            give(p, 0, 0)
        for p in order:
            add(p, 1, 0 if p in straight_out else 1)
            middle(p)

    @pl.when(plane == 2)
    def _():
        def share(p, lag_block):
            if p in straight_out:
                give_straight(p, lag_block)
            else:
                give(p, lag_block, 1 - lag_block)

        waiting = []
        for p in range(pieces):
            dealt(p, 0, 2)
            dealt(p, 1, 2)
            widen_into(lf, 2, held[p, 0, 2])
            widen_into(hf, 2, held[p, 1, 2])
            settle(held.at[p, 0, pl.ds(0, 3)], z_recv.at[p])
            widen_into(lf, 3, held[p, 0, 3])
            widen_into(hf, 3, held[p, 1, 3])
            widen_into(hf, 1, held[p, 1, 1])
            correlate_into(cf, lf, hf, 0, block, 2, groups)
            rounded(p, 0)
            share(p, 0)
            for other in waiting:
                share(other, 1)
            waiting = []
            settle(held.at[p, 1, 0], h_recv.at[p])
            widen_into(hf, 0, held[p, 1, 0])
            correlate_into(cf, lf, hf, 1, block, 2, groups)
            rounded(p, 1)
            if pieces - 1 - LATE <= p < pieces - 1:
                waiting.append(p)
            else:
                share(p, 1)
            correlate_into(cf, lf, hf, 3, block, 2, groups)
            rounded(p, 3)
            give(p, 3, 0)
            correlate_into(cf, lf, hf, 2, block, 2, groups)
            rounded(p, 2)
            back(cs.at[p, 2], p)
            middle(p)

    @pl.when(plane == 3)
    def _():
        for p in range(pieces):
            if p not in straight_in:
                for kind in range(2):
                    dealt(p, kind, 3)
                    lift(p, kind, 3, 2, z_recv)
        for p in range(pieces):
            settle(cin.at[p, 0], c_recv.at[p])
            back(cin.at[p, 0], p)
            middle(p)

    for c in range(chunks - 1):
        screen_sides(c)
    last = chunks - 1
    screen_own(last)

    @pl.when(jnp.logical_and(has_prev, has_next))
    def _():
        from_next(last, more)

    @pl.when(has_prev)
    def _():
        settle(side.at[1, last], side_recv.at[1, last])
        finish(side.at[1, last], wside[1], last)

    @pl.when(row == 0)
    def _():
        settle(side.at[0, last], side_recv.at[0, last])
        finish(side.at[0, last], wside[0], last)

    @pl.when(has_prev)
    def _():
        settle(polar, side_send.at[0])

    @pl.when(has_next)
    def _():
        settle(polar, side_send.at[1])
        u_copy.wait_send()

    others = pl.ds(0, k * (members - 1))
    settle(held.at[:, 0, 0, others], back_send)

    @pl.when(plane < 3)
    def _():
        for kind in range(2):
            settle(held.at[:, kind, 0, others], deal_send.at[kind])

    @pl.when(plane == 0)
    def _():
        settle(held.at[:, 0, 0], z_send)

    @pl.when(plane == 1)
    def _():
        settle(held.at[:, 0, pl.ds(0, 2)], z_send)
        settle(cs.at[:, 0], c_send)

    @pl.when(plane == 2)
    def _():
        settle(cs.at[:, pl.ds(0, 3)], c_send)

    @pl.when(plane == 3)
    def _():
        settle(held.at[:, 0, pl.ds(0, 2)], z_send)
        for kind in range(2):
            settle(held.at[pl.ds(0, pieces - STRAIGHT), kind, 0, others], deal_send.at[kind])


def fused(n, ns, lesser, greater, diag, upper):
    k, _, _, size, _ = lesser.shape
    members, energies, chunks = n // GROUPS, n * k, size // LANES
    block = members * k
    pieces = chunks * (size // members // TILE)
    bf, f32 = jnp.bfloat16, jnp.float32
    whole = (k, 2, size, size)
    piece = (block, 2, TILE, LANES)
    padded = energies + LAGS + STEPS
    dma = pltpu.SemaphoreType.DMA
    vmem = pl.BlockSpec(memory_space=pltpu.VMEM)
    hbm = pl.BlockSpec(memory_space=pltpu.HBM)
    return pl.pallas_call(
        functools.partial(kernel, n, ns),
        out_shape=jax.ShapeDtypeStruct(lesser.shape, bf),
        in_specs=[hbm] * 4,
        out_specs=vmem,
        scratch_shapes=[
            pltpu.VMEM(diag.shape, bf),
            pltpu.VMEM(upper.shape, bf),
            pltpu.VMEM(whole, bf),
            pltpu.VMEM(whole, bf),
            pltpu.VMEM((pieces, 2, GROUPS) + piece, bf),
            pltpu.VMEM((3, padded, TILE, LANES), f32),
            pltpu.VMEM((3, energies, TILE, LANES), f32),
            pltpu.VMEM(piece, f32),
            pltpu.VMEM((pieces,) + piece, f32),
            pltpu.VMEM((pieces, GROUPS) + piece, bf),
            pltpu.VMEM((pieces, 2) + piece, bf),
            pltpu.VMEM((STRAIGHT, k, 2, members * TILE, LANES), bf),
            pltpu.VMEM((chunks, k, 2, size, LANES), bf),
            pltpu.VMEM((2, chunks, k, 2, size, LANES), bf),
            pltpu.VMEM((size, size), bf),
            pltpu.VMEM((2, size, size), bf),
            pltpu.VMEM(whole, f32),
            dma((chunks + 2,)), dma((2,)), dma((2, pieces)), dma, dma((pieces,)), dma((pieces,)), dma,
            dma((pieces,)), dma((STRAIGHT,)), dma, dma((pieces,)), dma((2,)), dma((2, chunks)), dma, dma,
        ],
        compiler_params=pltpu.CompilerParams(
            collective_id=0, has_side_effects=True, vmem_limit_bytes=40 << 20
        ),
    )(*(pltpu.with_memory_space_constraint(x, pltpu.HBM) for x in (lesser, greater, diag, upper)))


def fits(n, ns, size, k):
    if n % GROUPS or size % LANES or size <= LANES or ns < 2:
        return False
    members = n // GROUPS
    if members < 2 or size % (members * TILE) or (members * k) % STEPS:
        return False
    stacks = size // members // TILE
    return 2 <= stacks and 2 * STRAIGHT <= size // LANES * stacks <= 16


def either(n, ns, lesser, greater, diag, upper):
    if fits(n, ns, lesser.shape[3], lesser.shape[0]):
        return fused(n, ns, lesser, greater, diag, upper)
    return per_device(lesser, greater, diag, upper)


def solution(mesh):
    placed = (
        P("energy", "space", None, None, None),
        P("energy", "space", None, None, None),
        P("space", None, None),
        P("space", None, None),
    )
    return jax.shard_map(
        functools.partial(either, mesh.shape["energy"], mesh.shape["space"]),
        mesh=mesh,
        in_specs=placed,
        out_specs=P("energy", "space", None, None, None),
        check_vma=False,
    )
```

time: 44.3 us -> 40.4 us (0.912)
  Pallas kernels: 43.4 us -> 39.2 us
    pallas_call x1, Pallas kernels: 43.4 us -> 39.2 us  [fused(): pl.pallas_call(functools.partial(kernel, n, ns), out_shape=jax.ShapeDtype...]
where the time goes in v2:
time: 40.4 us; the launch traced here: 40 us
  Pallas kernels  39.2 us (97%)
  local copies, waits for them, and re-layouts  0.8 us (2%)
    pallas_call x1, Pallas kernels, fused(): pl.pallas_call(functools.partial(kernel, n, ns), out_shape=jax.ShapeDtype...  39.2 us

profile of v2, /device:TPU:1, one launch (start us, length us, event | category | flops | bytes accessed | tf_op | source)
XLA Modules:
  0.0 40.0 jit_solution(9182726889107939607)
XLA Ops:
  0.0 39.2 %shard_map.46 = bf16[2,1,2,256,256]{4,3,2,1,0:T(8,128)(2,1)S(1)} custom-call(bf16[2,1,2,256,256]{4,3,2,1,0:T(8,128)(2,1)} %lesser.1, bf16[2,1,2,256,256]{4,3,2,1,0:T(8,128)(2,1)} %greater.1, bf16[1,256,256]{2,1,0:T(8,128)(2,1)} %diag_hbm.1, bf16[1,256,256]{2,1,0:T(8,128)(2,1)} %upper_hbm.1), custom_call_target="tpu_custom_call" | custom-call | tf_op jit(solution)/shard_map/pallas_call | solution.py:671
  39.2 0.8 %copy.6 = bf16[2,1,2,256,256]{4,3,2,1,0:T(8,128)(2,1)} copy(bf16[2,1,2,256,256]{4,3,2,1,0:T(8,128)(2,1)S(1)} %shard_map.46) | data formatting | bytes 1048576

commit v3 on v2

--- a/solution.py
+++ b/solution.py
@@ -114,9 +114,10 @@
 TILE = 16
 LANES = 128
 AHEAD = 4
-STRAIGHT = 2
-LATE = 1
-FIRST = 3
+STRAIGHT_IN = 2
+STRAIGHT_OUT = 3
+EARLY = 2
+FIRST = 2
 MESH = pl.DeviceIdType.MESH
 
 
@@ -171,8 +172,8 @@
 
 def kernel(
     n, ns, lesser, greater, diag_hbm, upper_hbm, out,
-    diag, upper, gv, ht, held, lf, hf, cf, own_sum, cs, cin, late, polar, side, uprev, wside, total,
-    local_sem, deal_send, deal_recv, z_send, z_recv, h_recv, c_send, c_recv, late_recv, back_send, back_recv,
+    diag, upper, gv, ht, held, lf, hf, cf, own_sum, own_low, cs, cin, late, polar, side, uprev, wside, total,
+    local_sem, deal_send, deal_recv, z_send, z_recv, h_recv, c_send, c_recv, m_recv, late_recv, back_send, back_recv,
     side_send, side_recv, u_send, u_recv,
 ):
     me = lax.axis_index("energy")
@@ -185,8 +186,10 @@
     plane, member = me // members, lax.rem(me, members)
     has_next = row < ns - 1
     has_prev = row > 0
-    straight_in = range(STRAIGHT)
-    straight_out = range(pieces - STRAIGHT, pieces)
+    straight_in = range(STRAIGHT_IN)
+    straight_out = range(pieces - STRAIGHT_OUT, pieces)
+    early = range(EARLY)
+    merged = range(EARLY, pieces - STRAIGHT_OUT)
 
     def column(level):
         return to_energy(level * members + member)
@@ -341,7 +344,8 @@
     load_upper.start()
     load_diag = pltpu.make_async_copy(diag_hbm, diag, local_sem.at[chunks + 1])
     load_diag.start()
-    lf[...] = jnp.zeros(lf.shape, jnp.float32)
+    for both in range(2):
+        lf[both] = jnp.zeros(lf.shape[1:], jnp.float32)
 
     @pl.when(has_next)
     def _():
@@ -364,6 +368,19 @@
             src_ref=cs.at[p, lag_block], dst_ref=cin.at[p, slot], send_sem=c_send,
             recv_sem=c_recv.at[p], device_id=column(lag_block), device_id_type=MESH,
         ).start()
+
+    def give_home(p, lag_block):
+        def push(step, carry):
+            peer = lax.rem(member + step, members)
+            pltpu.make_async_remote_copy(
+                src_ref=cs.at[p, lag_block, energies_of(peer)],
+                dst_ref=polar.at[p // stacks, :, :, share_rows(member, p), :],
+                send_sem=c_send, recv_sem=back_recv.at[p],
+                device_id=to_energy(lag_block * members + peer), device_id_type=MESH,
+            ).start()
+            return carry
+
+        lax.fori_loop(0, members, push, 0)
 
     def give_straight(p, lag_block):
         at = p - straight_out[0]
@@ -478,13 +495,6 @@
             u_copy.wait_recv()
             wside[1] = uprev[...].T
 
-    def middle(p):
-        c = (p - 1) // stacks - 1
-        if 0 <= c < chunks - 1 and (p - 1) % stacks == 0:
-            if c == 0:
-                couplers()
-            screen_own(c)
-
     def add(p, lag_block, slots):
         value = own_sum[p]
         if slots:
@@ -497,8 +507,16 @@
     def rounded(p, lag_block):
         cs[p, lag_block] = cf[...].astype(jnp.bfloat16)
 
-    early = list(range(max(0, stacks - 1)))
-    order = early + list(straight_out) + [p for p in range(pieces) if p not in early and p not in straight_out]
+    def give_middle(p):
+        pltpu.make_async_remote_copy(
+            src_ref=cs.at[p, 0], dst_ref=cin.at[p, 1], send_sem=c_send,
+            recv_sem=m_recv.at[p], device_id=column(1), device_id_type=MESH,
+        ).start()
+
+    def merge(p):
+        settle(cin.at[p, 1], m_recv.at[p])
+        cs[p, 0] = (own_low[p] + cin[p, 1].astype(jnp.float32)).astype(jnp.bfloat16)
+        give(p, 0, 0)
 
     @pl.when(plane == 0)
     def _():
@@ -510,12 +528,11 @@
             send(p)
         for p in range(pieces):
             dealt(p, 0, 0)
-            widen_into(lf, 0, held[p, 0, 0])
-            widen_into(hf, 0, held[p, 1, 0])
-            correlate_into(own_sum.at[p], lf, hf, 0, block, 0, 1)
-        for p in order:
-            add(p, 0, 1 if p in straight_out else 2)
-            middle(p)
+            widen_into(lf.at[0], 0, held[p, 0, 0])
+            widen_into(hf.at[0], 0, held[p, 1, 0])
+            correlate_into(own_sum.at[p], lf.at[0], hf.at[0], 0, block, 0, 1)
+        for p in (*early, *straight_out, *merged):
+            add(p, 0, 2 if p in early else 1)
 
     @pl.when(plane == 1)
     def _():
@@ -525,68 +542,79 @@
 
         for p in range(FIRST):
             send(p)
-        held_back = []
         for p in range(pieces):
             settle(held.at[p, 1, 0], h_recv.at[p])
             lift(p, 1, 0, 2, h_recv)
             if p + FIRST < pieces:
                 send(p + FIRST)
             dealt(p, 0, 1)
-            widen_into(lf, 1, held[p, 0, 1])
-            widen_into(hf, 1, held[p, 1, 1])
-            widen_into(hf, 0, held[p, 1, 0])
-            correlate_into(cf, lf, hf, 0, block, 1, 2)
-            rounded(p, 0)
-            if p in early or p in straight_out:
+            widen_into(lf.at[0], 1, held[p, 0, 1])
+            widen_into(hf.at[0], 1, held[p, 1, 1])
+            widen_into(hf.at[0], 0, held[p, 1, 0])
+            if p in merged:
+                correlate_into(own_low.at[p], lf.at[0], hf.at[0], 0, block, 1, 2)
+            else:
+                correlate_into(cf, lf.at[0], hf.at[0], 0, block, 1, 2)
+                rounded(p, 0)
                 give(p, 0, 0)
-            else:
-                held_back.append(p)
-            correlate_into(own_sum.at[p], lf, hf, 1, block, 1, 2)
-        for p in held_back:
-            give(p, 0, 0)
-        for p in order:
-            add(p, 1, 0 if p in straight_out else 1)
-            middle(p)
+            correlate_into(own_sum.at[p], lf.at[0], hf.at[0], 1, block, 1, 2)
+        for p in straight_out:
+            add(p, 1, 0)
+        for p in (*early, *merged):
+            if p + 1 in merged:
+                merge(p + 1)
+            add(p, 1, 1)
 
     @pl.when(plane == 2)
     def _():
         def share(p, lag_block):
             if p in straight_out:
                 give_straight(p, lag_block)
+            elif p in merged and lag_block == 0:
+                give_middle(p)
             else:
                 give(p, lag_block, 1 - lag_block)
 
-        waiting = []
-        for p in range(pieces):
+        def lags(p, lag_block):
+            correlate_into(cf, lf.at[p % 2], hf.at[p % 2], lag_block, block, 2, groups)
+            rounded(p, lag_block)
+
+        def lowest(p):
+            wide_l, wide_h = lf.at[p % 2], hf.at[p % 2]
             dealt(p, 0, 2)
             dealt(p, 1, 2)
-            widen_into(lf, 2, held[p, 0, 2])
-            widen_into(hf, 2, held[p, 1, 2])
+            widen_into(wide_l, 2, held[p, 0, 2])
+            widen_into(wide_h, 2, held[p, 1, 2])
             settle(held.at[p, 0, pl.ds(0, 3)], z_recv.at[p])
-            widen_into(lf, 3, held[p, 0, 3])
-            widen_into(hf, 3, held[p, 1, 3])
-            widen_into(hf, 1, held[p, 1, 1])
-            correlate_into(cf, lf, hf, 0, block, 2, groups)
-            rounded(p, 0)
+            widen_into(wide_l, 3, held[p, 0, 3])
+            widen_into(wide_h, 3, held[p, 1, 3])
+            widen_into(wide_h, 1, held[p, 1, 1])
+            lags(p, 0)
             share(p, 0)
-            for other in waiting:
-                share(other, 1)
-            waiting = []
+
+        def next_lowest(p):
             settle(held.at[p, 1, 0], h_recv.at[p])
-            widen_into(hf, 0, held[p, 1, 0])
-            correlate_into(cf, lf, hf, 1, block, 2, groups)
-            rounded(p, 1)
-            if pieces - 1 - LATE <= p < pieces - 1:
-                waiting.append(p)
-            else:
-                share(p, 1)
-            correlate_into(cf, lf, hf, 3, block, 2, groups)
-            rounded(p, 3)
-            give(p, 3, 0)
-            correlate_into(cf, lf, hf, 2, block, 2, groups)
-            rounded(p, 2)
+            widen_into(hf.at[p % 2], 0, held[p, 1, 0])
+            lags(p, 1)
+            share(p, 1)
+
+        def highest(p):
+            lags(p, 3)
+            give_home(p, 3)
+
+        def own_lags(p):
+            lags(p, 2)
             back(cs.at[p, 2], p)
-            middle(p)
+
+        for p in range(pieces - 1):
+            lowest(p)
+            if p:
+                for act in (next_lowest, highest, own_lags):
+                    act(p - 1)
+        lowest(pieces - 1)
+        for act in (next_lowest, highest, own_lags):
+            act(pieces - 2)
+            act(pieces - 1)
 
     @pl.when(plane == 3)
     def _():
@@ -595,11 +623,10 @@
                 for kind in range(2):
                     dealt(p, kind, 3)
                     lift(p, kind, 3, 2, z_recv)
-        for p in range(pieces):
-            settle(cin.at[p, 0], c_recv.at[p])
-            back(cin.at[p, 0], p)
-            middle(p)
-
+
+    couplers()
+    for c in range(chunks - 1):
+        screen_own(c)
     for c in range(chunks - 1):
         screen_sides(c)
     last = chunks - 1
@@ -629,10 +656,10 @@
         u_copy.wait_send()
 
     others = pl.ds(0, k * (members - 1))
-    settle(held.at[:, 0, 0, others], back_send)
 
     @pl.when(plane < 3)
     def _():
+        settle(held.at[:, 0, 0, others], back_send)
         for kind in range(2):
             settle(held.at[:, kind, 0, others], deal_send.at[kind])
 
@@ -653,7 +680,7 @@
     def _():
         settle(held.at[:, 0, pl.ds(0, 2)], z_send)
         for kind in range(2):
-            settle(held.at[pl.ds(0, pieces - STRAIGHT), kind, 0, others], deal_send.at[kind])
+            settle(held.at[pl.ds(0, pieces - STRAIGHT_IN), kind, 0, others], deal_send.at[kind])
 
 
 def fused(n, ns, lesser, greater, diag, upper):
@@ -679,20 +706,21 @@
             pltpu.VMEM(whole, bf),
             pltpu.VMEM(whole, bf),
             pltpu.VMEM((pieces, 2, GROUPS) + piece, bf),
-            pltpu.VMEM((3, padded, TILE, LANES), f32),
-            pltpu.VMEM((3, energies, TILE, LANES), f32),
+            pltpu.VMEM((2, 3, padded, TILE, LANES), f32),
+            pltpu.VMEM((2, 3, energies, TILE, LANES), f32),
             pltpu.VMEM(piece, f32),
+            pltpu.VMEM((pieces,) + piece, f32),
             pltpu.VMEM((pieces,) + piece, f32),
             pltpu.VMEM((pieces, GROUPS) + piece, bf),
             pltpu.VMEM((pieces, 2) + piece, bf),
-            pltpu.VMEM((STRAIGHT, k, 2, members * TILE, LANES), bf),
+            pltpu.VMEM((STRAIGHT_OUT, k, 2, members * TILE, LANES), bf),
             pltpu.VMEM((chunks, k, 2, size, LANES), bf),
             pltpu.VMEM((2, chunks, k, 2, size, LANES), bf),
             pltpu.VMEM((size, size), bf),
             pltpu.VMEM((2, size, size), bf),
             pltpu.VMEM(whole, f32),
             dma((chunks + 2,)), dma((2,)), dma((2, pieces)), dma, dma((pieces,)), dma((pieces,)), dma,
-            dma((pieces,)), dma((STRAIGHT,)), dma, dma((pieces,)), dma((2,)), dma((2, chunks)), dma, dma,
+            dma((pieces,)), dma((pieces,)), dma((STRAIGHT_OUT,)), dma, dma((pieces,)), dma((2,)), dma((2, chunks)), dma, dma,
         ],
         compiler_params=pltpu.CompilerParams(
             collective_id=0, has_side_effects=True, vmem_limit_bytes=40 << 20
@@ -707,7 +735,7 @@
     if members < 2 or size % (members * TILE) or (members * k) % STEPS:
         return False
     stacks = size // members // TILE
-    return 2 <= stacks and 2 * STRAIGHT <= size // LANES * stacks <= 16
+    return 2 <= stacks and EARLY + STRAIGHT_OUT < size // LANES * stacks <= 16
 
 
 def either(n, ns, lesser, greater, diag, upper):

time: 40.4 us -> 39 us (0.965)
  Pallas kernels: 39.2 us -> 38 us
    pallas_call x1, Pallas kernels: 39.2 us -> 38 us  [fused(): pl.pallas_call(functools.partial(kernel, n, ns), out_shape=jax.ShapeDtype...]
where the time goes in v3:
time: 39 us; the launch traced here: 38.9 us
  Pallas kernels  38 us (97%)
  local copies, waits for them, and re-layouts  0.8 us (2%)
    pallas_call x1, Pallas kernels, fused(): pl.pallas_call(functools.partial(kernel, n, ns), out_shape=jax.ShapeDtype...  38 us
    unnamed x1, local copies, waits for them, and re-layouts  0.8 us

profile of v3, /device:TPU:1, one launch (start us, length us, event | category | flops | bytes accessed | tf_op | source)
XLA Modules:
  0.0 38.9 jit_solution(3932284444491366678)
XLA Ops:
  0.0 38.0 %shard_map.46 = bf16[2,1,2,256,256]{4,3,2,1,0:T(8,128)(2,1)S(1)} custom-call(bf16[2,1,2,256,256]{4,3,2,1,0:T(8,128)(2,1)} %lesser.1, bf16[2,1,2,256,256]{4,3,2,1,0:T(8,128)(2,1)} %greater.1, bf16[1,256,256]{2,1,0:T(8,128)(2,1)} %diag_hbm.1, bf16[1,256,256]{2,1,0:T(8,128)(2,1)} %upper_hbm.1), custom_call_target="tpu_custom_call" | custom-call | tf_op jit(solution)/shard_map/pallas_call | solution.py:698
  38.1 0.8 %copy.6 = bf16[2,1,2,256,256]{4,3,2,1,0:T(8,128)(2,1)} copy(bf16[2,1,2,256,256]{4,3,2,1,0:T(8,128)(2,1)S(1)} %shard_map.46) | data formatting | bytes 1048576
